TPU v7x, 32 devices: a whole 2x2x4 slice. The times are simulated.
32 devices in a mesh: wide: 8 (over y, x, core), narrow: 4 (over z).
Axes of the slice: x: 2, y: 2, z: 4, core: 2. Of those that a mesh axis runs over, the one named last changes fastest.
Arguments:
- hamiltonian_tiles: float32 [12288, 6144], P('wide', 'narrow'), may hold values from -0.0546875 to 0.0546875
- row_columns: int32 [8, 4], P('wide'), may hold values from 0 to 7, as said below
- start_vectors: float32 [12288, 128], P(('wide', 'narrow')), may hold values from -60 to 60
Outputs:
- new_vectors: float32 [12288, 128], P(('wide', 'narrow'))
Inputs may be any that keep to these rules, and one draw needn't show every extreme that they name: For block row r = w + j // 4, row_columns[w, j] = (r + d) mod 8, with d = 0 where j % 4 = 0 and, for the other tiles of that block row, distinct d between 1 and 7; a block's mirror may also be stored.
All inputs are finite; a program needn't handle non-finite values.
Results may differ from a plain program's by a relative error of at most 0.0003.
Values sent between devices are 32-bit elements; how exact they have to be, the bound alone decides.
A program may use at most 64 MiB of HBM per device.

v0:
```python
import jax
import jax.numpy as jnp
from jax import lax
from jax.sharding import PartitionSpec as P

ITERS = 2
NS_STEPS = 5


def orthonormalize(product, gram, total_rows):
    width = gram.shape[0]
    identity = jnp.eye(width, dtype=jnp.float32)
    scale = jnp.sqrt(jnp.sum(gram * gram) + 1e-06)
    current = gram / scale
    inverse = identity
    for repeat in range(NS_STEPS):
        middle = 1.5 * identity - 0.5 * jnp.dot(inverse, current, precision=lax.Precision.HIGHEST)
        current = jnp.dot(current, middle, precision=lax.Precision.HIGHEST)
        inverse = jnp.dot(middle, inverse, precision=lax.Precision.HIGHEST)
    return jnp.dot(product, inverse, precision=lax.Precision.HIGHEST) * jnp.sqrt(total_rows / scale)


def on_device(hamiltonian_tiles, row_columns, start_vectors):
    narrow_count = lax.axis_size("narrow")
    wide_count = lax.axis_size("wide")
    my_index = lax.axis_index("narrow")
    order_tile = hamiltonian_tiles.shape[0]
    slice_rows = start_vectors.shape[0]
    width = start_vectors.shape[1]
    per_row = order_tile // slice_rows
    rows_group = narrow_count // per_row
    my_block = my_index // per_row
    columns_row = row_columns[0]
    column_group = columns_row // rows_group
    column_place = columns_row % rows_group
    my_column_place = column_place[my_index]
    sender_block = jnp.arange(narrow_count, dtype=jnp.int32) // per_row
    back_weight = (
        (column_group[:, None] == jnp.arange(wide_count, dtype=jnp.int32)[None, :])
        & (column_place[:, None] == my_block)
    ).astype(jnp.float32)
    own_weight = (sender_block == my_block).astype(jnp.float32)
    total_rows = float(wide_count * rows_group * order_tile)
    vectors = start_vectors
    for repeat in range(ITERS):
        slices = lax.all_gather(vectors, "wide", axis=0, tiled=True)
        picked = jnp.take(slices.reshape(wide_count, slice_rows, width), column_group, axis=0)
        gathered_rows = lax.all_gather(vectors, "narrow", axis=0, tiled=True)
        got_column = lax.all_to_all(picked, "narrow", split_axis=0, concat_axis=0, tiled=True)
        row_block = lax.dynamic_index_in_dim(
            gathered_rows.reshape(rows_group, order_tile, width), my_block, 0, keepdims=False
        )
        column_block = lax.dynamic_index_in_dim(
            got_column.reshape(rows_group, order_tile, width), my_column_place, 0, keepdims=False
        )
        direct = jnp.dot(hamiltonian_tiles, column_block, precision=lax.Precision.HIGHEST)
        transposed = lax.dot_general(
            hamiltonian_tiles, row_block, (((0,), (0,)), ((), ())), precision=lax.Precision.HIGHEST
        )
        transposed_spread = transposed.reshape(1, per_row, slice_rows, width).reshape(
            narrow_count, slice_rows, width
        )
        direct_spread = direct.reshape(1, per_row, slice_rows, width).reshape(
            narrow_count, slice_rows, width
        )
        arrived, direct_pieces = (
            lax.all_to_all(transposed_spread, "narrow", split_axis=0, concat_axis=0, tiled=True),
            lax.all_to_all(direct_spread, "narrow", split_axis=0, concat_axis=0, tiled=True),
        )
        direct_part = jnp.einsum(
            "n,nsk->sk", own_weight, direct_pieces, precision=lax.Precision.HIGHEST
        )
        placed = jnp.einsum("nb,nsk->bsk", back_weight, arrived, precision=lax.Precision.HIGHEST)
        moved_part = lax.psum_scatter(
            placed.reshape(wide_count * slice_rows, width), "wide", scatter_dimension=0, tiled=True
        )
        product = direct_part + moved_part
        local_gram = lax.dot_general(
            product, product, (((0,), (0,)), ((), ())), precision=lax.Precision.HIGHEST
        )
        gram = lax.psum(local_gram, ("wide", "narrow"))
        vectors = orthonormalize(product, gram, total_rows)
    return vectors


def solution(mesh):
    return jax.shard_map(
        on_device,
        mesh=mesh,
        in_specs=(P("wide", "narrow"), P("wide", None), P(("wide", "narrow"), None)),
        out_specs=P(("wide", "narrow"), None),
        check_vma=False,
    )
```

profile of v0, /device:TPU:1, one launch (start us, length us, event | category | flops | bytes accessed | tf_op | source)
XLA Modules:
  0.0 499.5 jit_solution(15545345940733565304)
XLA Ops:
  7.3 18.2 %all_gather.13 = f32[1536,128]{1,0:T(8,128)S(1)} all-gather(f32[384,128]{1,0:T(8,128)} %param.7), channel_id=1, replica_groups=mesh['wide'=8,'narrow'=4] {'narrow'}, dimensions={0}, use_global_device_ids=true | all-gather | bytes 983040 | tf_op jit(solution)/shard_map/all_gather | solution.py:48
  25.5 18.1 %fusion.41 = f32[1536,128]{1,0:T(8,128)} fusion(f32[1536,1536]{1,0:T(8,128)} %param.5, f32[1536,128]{1,0:T(8,128)S(1)} %all_gather.13), kind=kOutput, calls=%fused_computation.71 | convolution fusion | flops 3623878656 | bytes 11010048 | tf_op jit(solution)/shard_map/dot_general | solution.py:57
  43.6 4.0 all-to-all-start.2
  47.7 2.0 gather_fusion
  50.7 16.3 %all-to-all-done.2 = f32[4,384,128]{2,1,0:T(8,128)S(1)} async-done(((f32[4,384,128]{2,1,0:T(8,128)}), f32[4,384,128]{2,1,0:T(8,128)S(1)}, u32[]{:S(2)}, u32[]{:S(2)}) %all-to-all-start.2) | async-done | bytes 786464 | tf_op jit(solution)/shard_map/all_to_all | solution.py:67
  66.9 3.5 all-to-all-start
  70.5 1.5 fusion.12
  72.0 1.4 copy.12
  73.6 16.4 %all-to-all-done = f32[4,384,128]{2,1,0:T(8,128)S(1)} async-done(((f32[4,384,128]{2,1,0:T(8,128)}), f32[4,384,128]{2,1,0:T(8,128)S(1)}, u32[]{:S(2)}, u32[]{:S(2)}) %all-to-all-start) | async-done | bytes 786464 | tf_op jit(solution)/shard_map/all_to_all | solution.py:49
  90.0 10.4 %fusion.40 = f32[128,1536]{1,0:T(8,128)S(1)} fusion(f32[1536,128]{1,0:T(8,128)S(1)} %bitcast.108, f32[1536,1536]{1,0:T(8,128)} %param.5), kind=kOutput, calls=%fused_computation.70 | convolution fusion | flops 3623878656 | bytes 11010048 | tf_op jit(solution)/shard_map/dot_general | solution.py:56
  100.5 21.5 %all_to_all.30 = f32[4,384,128]{1,2,0:T(8,128)S(1)} all-to-all(f32[4,384,128]{1,2,0:T(8,128)S(1)} %bitcast.106), channel_id=1, replica_groups=mesh['wide'=8,'narrow'=4] {'narrow'}, dimensions={0} | all-to-all | bytes 1572864 | tf_op jit(solution)/shard_map/all_to_all | solution.py:68
  124.2 1.1 fusion.42
  125.4 121.8 %all-reduce.3.cloned.1.call-done = f32[128,128]{1,0:T(8,128)} async-done(((f32[128,128]{1,0:T(8,128)}), f32[128,128]{1,0:T(8,128)}) %all-reduce.3.cloned.1.call-update) | async-done | bytes 65552 | tf_op jit(solution)/shard_map/psum | solution.py:81
  247.2 1.5 multiply_reduce_fusion.1
  249.3 1.0 fusion.9
  250.5 1.0 fusion.16
  255.0 17.0 %all_gather.15 = f32[1536,128]{1,0:T(8,128)S(1)} all-gather(f32[384,128]{1,0:T(8,128)} %convolution_multiply_fusion.1), channel_id=1, replica_groups=mesh['wide'=8,'narrow'=4] {'narrow'}, dimensions={0}, use_global_device_ids=true | all-gather | bytes 983040 | tf_op jit(solution)/shard_map/all_gather | solution.py:48
  272.0 8.6 %convolution_bitcast_fusion = f32[1536,128]{0,1:T(8,128)S(1)} fusion(f32[1536,128]{1,0:T(8,128)S(1)} %all_gather.15, f32[1536,1536]{1,0:T(8,128)} %param.5), kind=kOutput, calls=%fused_computation.2 | convolution fusion | flops 3623878656 | bytes 11010048 | tf_op jit(solution)/shard_map/dot_general | solution.py:57
  280.6 1.1 copy.21
  281.7 4.1 all-to-all-start.5
  285.8 2.0 gather_fusion.1
  288.8 16.7 %all-to-all-done.5 = f32[4,384,128]{2,1,0:T(8,128)S(1)} async-done(((f32[4,384,128]{2,1,0:T(8,128)}), f32[4,384,128]{2,1,0:T(8,128)S(1)}, u32[]{:S(2)}, u32[]{:S(2)}) %all-to-all-start.5) | async-done | bytes 786464 | tf_op jit(solution)/shard_map/all_to_all | solution.py:67
  305.5 3.5 all-to-all-start.3
  309.3 1.5 fusion.10
  310.7 1.4 copy.16
  312.2 16.4 %all-to-all-done.3 = f32[4,384,128]{2,1,0:T(8,128)S(1)} async-done(((f32[4,384,128]{2,1,0:T(8,128)}), f32[4,384,128]{2,1,0:T(8,128)S(1)}, u32[]{:S(2)}, u32[]{:S(2)}) %all-to-all-start.3) | async-done | bytes 786464 | tf_op jit(solution)/shard_map/all_to_all | solution.py:49
  328.6 10.4 %fusion.50 = f32[128,1536]{1,0:T(8,128)S(1)} fusion(f32[1536,128]{1,0:T(8,128)S(1)} %bitcast.109, f32[1536,1536]{1,0:T(8,128)} %param.5), kind=kOutput, calls=%fused_computation.80 | convolution fusion | flops 3623878656 | bytes 11010048 | tf_op jit(solution)/shard_map/dot_general | solution.py:56
  339.1 21.5 %all_to_all.31 = f32[4,384,128]{1,2,0:T(8,128)S(1)} all-to-all(f32[4,384,128]{1,2,0:T(8,128)S(1)} %bitcast.107), channel_id=1, replica_groups=mesh['wide'=8,'narrow'=4] {'narrow'}, dimensions={0} | all-to-all | bytes 1572864 | tf_op jit(solution)/shard_map/all_to_all | solution.py:68
  362.8 1.1 fusion.51
  363.9 120.9 %all-reduce.5.cloned.1.call-done = f32[128,128]{1,0:T(8,128)} async-done(((f32[128,128]{1,0:T(8,128)}), f32[128,128]{1,0:T(8,128)}) %all-reduce.5.cloned.1.call-update) | async-done | bytes 65552 | tf_op jit(solution)/shard_map/psum | solution.py:81
  484.8 1.5 multiply_reduce_fusion
  488.2 1.0 fusion.17
  (58 shorter events, 15.6 us)
Async XLA Ops:
  6.5 41.1 %all-gather.3.cloned.1.call-start = ((), (), s32[]{:S(2)}) async-start(), calls=%async_computation.8 | async-start | bytes 1769472 | tf_op jit(solution)/shard_map/all_gather | solution.py:46
  25.5 22.1 %copy-start = (s32[1,4]{1,0:T(1,128)S(1)}, s32[1,4]{1,0:T(1,128)}, u32[]{:S(2)}) copy-start(s32[1,4]{1,0:T(1,128)} %param.6) | copy-start | bytes 52
  43.6 23.4 %all-to-all-start.2 = ((f32[4,384,128]{2,1,0:T(8,128)}), f32[4,384,128]{2,1,0:T(8,128)S(1)}, u32[]{:S(2)}, u32[]{:S(2)}) async-start(f32[4,384,128]{2,1,0:T(8,128)} %bitcast.9), calls=%async_computation.2 | async-start | bytes 1572864 | tf_op jit(solution)/shard_map/all_to_all | solution.py:67
  66.9 23.1 %all-to-all-start = ((f32[4,384,128]{2,1,0:T(8,128)}), f32[4,384,128]{2,1,0:T(8,128)S(1)}, u32[]{:S(2)}, u32[]{:S(2)}) async-start(f32[4,384,128]{2,1,0:T(8,128)} %broadcast_select_fusion.1), calls=%async_computation | async-start | bytes 1572864 | tf_op jit(solution)/shard_map/all_to_all | solution.py:49
  70.4 52.8 %reduce-scatter.3.cloned.1.call-start = ((), (), s32[]{:S(2)}) async-start(), calls=%async_computation.9 | async-start | bytes 1769472 | tf_op jit(solution)/shard_map/reduce_scatter | solution.py:74
  73.4 173.8 %all-reduce.3.cloned.1.call-start = ((), (), s32[]{:S(2)}) async-start(), calls=%async_computation.10 | async-start | bytes 131072 | tf_op jit(solution)/shard_map/psum | solution.py:81
  125.3 160.5 %all-gather.5.cloned.1.call-start = ((), (), s32[]{:S(2)}) async-start(), calls=%async_computation.11 | async-start | bytes 1769472 | tf_op jit(solution)/shard_map/all_gather | solution.py:46
  281.7 23.8 %all-to-all-start.5 = ((f32[4,384,128]{2,1,0:T(8,128)}), f32[4,384,128]{2,1,0:T(8,128)S(1)}, u32[]{:S(2)}, u32[]{:S(2)}) async-start(f32[4,384,128]{2,1,0:T(8,128)} %bitcast.17), calls=%async_computation.6 | async-start | bytes 1572864 | tf_op jit(solution)/shard_map/all_to_all | solution.py:67
  305.5 23.1 %all-to-all-start.3 = ((f32[4,384,128]{2,1,0:T(8,128)}), f32[4,384,128]{2,1,0:T(8,128)S(1)}, u32[]{:S(2)}, u32[]{:S(2)}) async-start(f32[4,384,128]{2,1,0:T(8,128)} %broadcast_select_fusion), calls=%async_computation.4 | async-start | bytes 1572864 | tf_op jit(solution)/shard_map/all_to_all | solution.py:49
  309.0 52.8 %reduce-scatter.5.cloned.1.call-start = ((), (), s32[]{:S(2)}) async-start(), calls=%async_computation.12 | async-start | bytes 1769472 | tf_op jit(solution)/shard_map/reduce_scatter | solution.py:74
  312.2 172.6 %all-reduce.5.cloned.1.call-start = ((), (), s32[]{:S(2)}) async-start(), calls=%async_computation.13 | async-start | bytes 131072 | tf_op jit(solution)/shard_map/psum | solution.py:81
Sparse Core Ops, SparseCore 0:
  9.2 28.0 all-gather.2
  74.5 40.6 reduce-scatter.2
  125.5 121.6 all-reduce.2
  255.1 25.3 all-gather.4
  312.8 39.4 reduce-scatter.4
  364.0 120.7 all-reduce.4
where the time goes:
time: 500 us
  waiting for transfers between devices  309 us (62%)
  blocking collectives  78.3 us (16%)
  matrix products  65.2 us (13%)
  starting transfers between devices  15.8 us (3%)
  between operations  15.4 us (3%)
  local copies, waits for them, and re-layouts  8.74 us (2%)
  other arithmetic  6.83 us (1%)
    psum x2, waiting for transfers between devices, on_device(): gram = lax.psum(local_gram, ('wide', 'narrow'))  243 us
    all_to_all x2, blocking collectives, on_device(): lax.all_to_all(direct_spread, 'narrow', split_axis=0, concat_axis=0, tile...  43.1 us
    all_gather x2, blocking collectives, on_device(): gathered_rows = lax.all_gather(vectors, 'narrow', axis=0, tiled=True)  35.2 us
    all_to_all x2, waiting for transfers between devices, on_device(): lax.all_to_all(transposed_spread, 'narrow', split_axis=0, concat_axis=0,...  32.9 us
    all_to_all x2, waiting for transfers between devices, on_device(): lax.all_to_all(picked, 'narrow', split_axis=0, concat_axis=0, tiled=True)  32.8 us
    dot_general x2, matrix products, on_device(): lax.dot_general(hamiltonian_tiles, row_block, (((0,), (0,)), ((), ())), p...  26.6 us
    dot_general x2, matrix products, on_device(): jnp.dot(hamiltonian_tiles, column_block, precision=lax.Precision.HIGHEST)  20.9 us
  transfers between devices with their start and end apart: 10, of which 6 were waited for; matrix products, arithmetic and copies ran while one was open for 13% of the time, Pallas kernels for 0%

commit v1 on v0

--- a/solution.py
+++ b/solution.py
@@ -78,7 +78,7 @@
         local_gram = lax.dot_general(
             product, product, (((0,), (0,)), ((), ())), precision=lax.Precision.HIGHEST
         )
-        gram = lax.psum(local_gram, ("wide", "narrow"))
+        gram = lax.psum(lax.psum(local_gram, "narrow"), "wide")
         vectors = orthonormalize(product, gram, total_rows)
     return vectors
 

time: 500 us -> 433 us (0.87)
  waiting for transfers between devices: 309 us -> 242 us
    psum x2 -> x4, waiting for transfers between devices: 243 us -> 178 us  [on_device(): gram = lax.psum(lax.psum(local_gram, 'narrow'), 'wide')]
  transfers between devices with their start and end apart: 10 -> 12, of which waited for: 6 -> 8; matrix products, arithmetic and copies ran while one was open for 13% -> 15% of each run, Pallas kernels for 0% -> 0%
where the time goes in v1:
time: 433 us; the launch traced here: 431 us
  waiting for transfers between devices  242 us (56%)
  blocking collectives  77.1 us (18%)
  matrix products  65 us (15%)
  starting transfers between devices  16 us (4%)
  between operations  15.5 us (4%)
  local copies, waits for them, and re-layouts  8.74 us (2%)
  other arithmetic  6.83 us (2%)
    psum x4, waiting for transfers between devices, on_device(): gram = lax.psum(lax.psum(local_gram, 'narrow'), 'wide')  178 us
    all_to_all x2, blocking collectives, on_device(): lax.all_to_all(direct_spread, 'narrow', split_axis=0, concat_axis=0, tile...  43 us
    all_gather x2, blocking collectives, on_device(): gathered_rows = lax.all_gather(vectors, 'narrow', axis=0, tiled=True)  34.1 us
    all_to_all x2, waiting for transfers between devices, on_device(): lax.all_to_all(picked, 'narrow', split_axis=0, concat_axis=0, tiled=True)  31.8 us
    all_to_all x2, waiting for transfers between devices, on_device(): lax.all_to_all(transposed_spread, 'narrow', split_axis=0, concat_axis=0,...  30.6 us
    dot_general x2, matrix products, on_device(): lax.dot_general(hamiltonian_tiles, row_block, (((0,), (0,)), ((), ())), p...  26.4 us
    dot_general x2, matrix products, on_device(): jnp.dot(hamiltonian_tiles, column_block, precision=lax.Precision.HIGHEST)  20.9 us
  transfers between devices with their start and end apart: 12, of which 8 were waited for; matrix products, arithmetic and copies ran while one was open for 15% of the time, Pallas kernels for 0%

profile of v1, /device:TPU:1, one launch (start us, length us, event | category | flops | bytes accessed | tf_op | source)
XLA Modules:
  0.0 430.8 jit_solution(5624447132639914177)
XLA Ops:
  7.3 18.2 %all_gather.13 = f32[1536,128]{1,0:T(8,128)S(1)} all-gather(f32[384,128]{1,0:T(8,128)} %param.7), channel_id=1, replica_groups=mesh['wide'=8,'narrow'=4] {'narrow'}, dimensions={0}, use_global_device_ids=true | all-gather | bytes 983040 | tf_op jit(solution)/shard_map/all_gather | solution.py:48
  25.5 18.1 %fusion.41 = f32[1536,128]{1,0:T(8,128)} fusion(f32[1536,1536]{1,0:T(8,128)} %param.5, f32[1536,128]{1,0:T(8,128)S(1)} %all_gather.13), kind=kOutput, calls=%fused_computation.71 | convolution fusion | flops 3623878656 | bytes 11010048 | tf_op jit(solution)/shard_map/dot_general | solution.py:57
  43.6 4.0 all-to-all-start.2
  47.7 2.0 gather_fusion
  50.7 16.3 %all-to-all-done.2 = f32[4,384,128]{2,1,0:T(8,128)S(1)} async-done(((f32[4,384,128]{2,1,0:T(8,128)}), f32[4,384,128]{2,1,0:T(8,128)S(1)}, u32[]{:S(2)}, u32[]{:S(2)}) %all-to-all-start.2) | async-done | bytes 786464 | tf_op jit(solution)/shard_map/all_to_all | solution.py:67
  66.9 3.5 all-to-all-start
  70.5 1.5 fusion.12
  72.0 1.4 copy.12
  73.6 16.4 %all-to-all-done = f32[4,384,128]{2,1,0:T(8,128)S(1)} async-done(((f32[4,384,128]{2,1,0:T(8,128)}), f32[4,384,128]{2,1,0:T(8,128)S(1)}, u32[]{:S(2)}, u32[]{:S(2)}) %all-to-all-start) | async-done | bytes 786464 | tf_op jit(solution)/shard_map/all_to_all | solution.py:49
  90.0 10.4 %fusion.40 = f32[128,1536]{1,0:T(8,128)S(1)} fusion(f32[1536,128]{1,0:T(8,128)S(1)} %bitcast.108, f32[1536,1536]{1,0:T(8,128)} %param.5), kind=kOutput, calls=%fused_computation.70 | convolution fusion | flops 3623878656 | bytes 11010048 | tf_op jit(solution)/shard_map/dot_general | solution.py:56
  100.5 21.5 %all_to_all.30 = f32[4,384,128]{1,2,0:T(8,128)S(1)} all-to-all(f32[4,384,128]{1,2,0:T(8,128)S(1)} %bitcast.106), channel_id=1, replica_groups=mesh['wide'=8,'narrow'=4] {'narrow'}, dimensions={0} | all-to-all | bytes 1572864 | tf_op jit(solution)/shard_map/all_to_all | solution.py:68
  124.2 1.1 fusion.42
  125.4 32.8 %all-reduce.5.cloned.1.call-done = f32[128,128]{1,0:T(8,128)} async-done(((f32[128,128]{1,0:T(8,128)}), f32[128,128]{1,0:T(8,128)}) %all-reduce.5.cloned.1.call-update) | async-done | bytes 65552 | tf_op jit(solution)/shard_map/psum | solution.py:81
  158.2 57.0 %all-reduce.7.cloned.1.call-done = f32[128,128]{1,0:T(8,128)} async-done(((f32[128,128]{1,0:T(8,128)}), f32[128,128]{1,0:T(8,128)}) %all-reduce.7.cloned.1.call-update) | async-done | bytes 65552 | tf_op jit(solution)/shard_map/psum | solution.py:81
  215.2 1.5 multiply_reduce_fusion.1
  218.6 1.0 fusion.16
  223.1 15.8 %all_gather.15 = f32[1536,128]{1,0:T(8,128)S(1)} all-gather(f32[384,128]{1,0:T(8,128)} %convolution_multiply_fusion.1), channel_id=1, replica_groups=mesh['wide'=8,'narrow'=4] {'narrow'}, dimensions={0}, use_global_device_ids=true | all-gather | bytes 983040 | tf_op jit(solution)/shard_map/all_gather | solution.py:48
  238.9 8.3 %convolution_bitcast_fusion = f32[1536,128]{0,1:T(8,128)S(1)} fusion(f32[1536,128]{1,0:T(8,128)S(1)} %all_gather.15, f32[1536,1536]{1,0:T(8,128)} %param.5), kind=kOutput, calls=%fused_computation.2 | convolution fusion | flops 3623878656 | bytes 11010048 | tf_op jit(solution)/shard_map/dot_general | solution.py:57
  247.2 1.1 copy.21
  248.4 4.3 all-to-all-start.5
  252.6 2.0 gather_fusion.1
  255.7 14.4 %all-to-all-done.5 = f32[4,384,128]{2,1,0:T(8,128)S(1)} async-done(((f32[4,384,128]{2,1,0:T(8,128)}), f32[4,384,128]{2,1,0:T(8,128)S(1)}, u32[]{:S(2)}, u32[]{:S(2)}) %all-to-all-start.5) | async-done | bytes 786464 | tf_op jit(solution)/shard_map/all_to_all | solution.py:67
  270.0 3.5 all-to-all-start.3
  273.8 1.5 fusion.10
  275.3 1.4 copy.16
  276.8 15.4 %all-to-all-done.3 = f32[4,384,128]{2,1,0:T(8,128)S(1)} async-done(((f32[4,384,128]{2,1,0:T(8,128)}), f32[4,384,128]{2,1,0:T(8,128)S(1)}, u32[]{:S(2)}, u32[]{:S(2)}) %all-to-all-start.3) | async-done | bytes 786464 | tf_op jit(solution)/shard_map/all_to_all | solution.py:49
  292.1 10.5 %fusion.50 = f32[128,1536]{1,0:T(8,128)S(1)} fusion(f32[1536,128]{1,0:T(8,128)S(1)} %bitcast.109, f32[1536,1536]{1,0:T(8,128)} %param.5), kind=kOutput, calls=%fused_computation.80 | convolution fusion | flops 3623878656 | bytes 11010048 | tf_op jit(solution)/shard_map/dot_general | solution.py:56
  302.7 21.5 %all_to_all.31 = f32[4,384,128]{1,2,0:T(8,128)S(1)} all-to-all(f32[4,384,128]{1,2,0:T(8,128)S(1)} %bitcast.107), channel_id=1, replica_groups=mesh['wide'=8,'narrow'=4] {'narrow'}, dimensions={0} | all-to-all | bytes 1572864 | tf_op jit(solution)/shard_map/all_to_all | solution.py:68
  326.3 1.1 fusion.51
  327.5 31.4 %all-reduce.9.cloned.1.call-done = f32[128,128]{1,0:T(8,128)} async-done(((f32[128,128]{1,0:T(8,128)}), f32[128,128]{1,0:T(8,128)}) %all-reduce.9.cloned.1.call-update) | async-done | bytes 65552 | tf_op jit(solution)/shard_map/psum | solution.py:81
  358.9 57.2 %all-reduce.11.cloned.1.call-done = f32[128,128]{1,0:T(8,128)} async-done(((f32[128,128]{1,0:T(8,128)}), f32[128,128]{1,0:T(8,128)}) %all-reduce.11.cloned.1.call-update) | async-done | bytes 65552 | tf_op jit(solution)/shard_map/psum | solution.py:81
  416.1 1.5 multiply_reduce_fusion
  (64 shorter events, 17.8 us)
Async XLA Ops:
  6.5 41.1 %all-gather.3.cloned.1.call-start = ((), (), s32[]{:S(2)}) async-start(), calls=%async_computation.8 | async-start | bytes 1769472 | tf_op jit(solution)/shard_map/all_gather | solution.py:46
  25.5 22.1 %copy-start = (s32[1,4]{1,0:T(1,128)S(1)}, s32[1,4]{1,0:T(1,128)}, u32[]{:S(2)}) copy-start(s32[1,4]{1,0:T(1,128)} %param.6) | copy-start | bytes 52
  43.6 23.4 %all-to-all-start.2 = ((f32[4,384,128]{2,1,0:T(8,128)}), f32[4,384,128]{2,1,0:T(8,128)S(1)}, u32[]{:S(2)}, u32[]{:S(2)}) async-start(f32[4,384,128]{2,1,0:T(8,128)} %bitcast.9), calls=%async_computation.2 | async-start | bytes 1572864 | tf_op jit(solution)/shard_map/all_to_all | solution.py:67
  66.9 23.1 %all-to-all-start = ((f32[4,384,128]{2,1,0:T(8,128)}), f32[4,384,128]{2,1,0:T(8,128)S(1)}, u32[]{:S(2)}, u32[]{:S(2)}) async-start(f32[4,384,128]{2,1,0:T(8,128)} %broadcast_select_fusion.1), calls=%async_computation | async-start | bytes 1572864 | tf_op jit(solution)/shard_map/all_to_all | solution.py:49
  70.4 52.8 %reduce-scatter.3.cloned.1.call-start = ((), (), s32[]{:S(2)}) async-start(), calls=%async_computation.9 | async-start | bytes 1769472 | tf_op jit(solution)/shard_map/reduce_scatter | solution.py:74
  73.4 84.7 %all-reduce.5.cloned.1.call-start = ((), (), s32[]{:S(2)}) async-start(), calls=%async_computation.10 | async-start | bytes 131072 | tf_op jit(solution)/shard_map/psum | solution.py:81
  125.3 89.9 %all-reduce.7.cloned.1.call-start = ((), (), s32[]{:S(2)}) async-start(), calls=%async_computation.11 | async-start | bytes 131072 | tf_op jit(solution)/shard_map/psum | solution.py:81
  158.2 94.5 %all-gather.5.cloned.1.call-start = ((), (), s32[]{:S(2)}) async-start(), calls=%async_computation.12 | async-start | bytes 1769472 | tf_op jit(solution)/shard_map/all_gather | solution.py:46
  248.4 21.7 %all-to-all-start.5 = ((f32[4,384,128]{2,1,0:T(8,128)}), f32[4,384,128]{2,1,0:T(8,128)S(1)}, u32[]{:S(2)}, u32[]{:S(2)}) async-start(f32[4,384,128]{2,1,0:T(8,128)} %bitcast.17), calls=%async_computation.6 | async-start | bytes 1572864 | tf_op jit(solution)/shard_map/all_to_all | solution.py:67
  270.0 22.1 %all-to-all-start.3 = ((f32[4,384,128]{2,1,0:T(8,128)}), f32[4,384,128]{2,1,0:T(8,128)S(1)}, u32[]{:S(2)}, u32[]{:S(2)}) async-start(f32[4,384,128]{2,1,0:T(8,128)} %broadcast_select_fusion), calls=%async_computation.4 | async-start | bytes 1572864 | tf_op jit(solution)/shard_map/all_to_all | solution.py:49
  273.5 51.8 %reduce-scatter.5.cloned.1.call-start = ((), (), s32[]{:S(2)}) async-start(), calls=%async_computation.13 | async-start | bytes 1769472 | tf_op jit(solution)/shard_map/reduce_scatter | solution.py:74
  276.7 82.1 %all-reduce.9.cloned.1.call-start = ((), (), s32[]{:S(2)}) async-start(), calls=%async_computation.14 | async-start | bytes 131072 | tf_op jit(solution)/shard_map/psum | solution.py:81
  327.4 88.7 %all-reduce.11.cloned.1.call-start = ((), (), s32[]{:S(2)}) async-start(), calls=%async_computation.15 | async-start | bytes 131072 | tf_op jit(solution)/shard_map/psum | solution.py:81
Sparse Core Ops, SparseCore 0:
  9.2 28.0 all-gather.2
  74.5 40.6 reduce-scatter.2
  125.5 32.6 all-reduce.4
  161.1 54.1 all-reduce.6
  223.2 26.1 all-gather.4
  277.3 40.9 reduce-scatter.4
  327.5 31.2 all-reduce.8
  361.9 54.1 all-reduce.10
